TPU v7x, 128 devices: a whole 4x4x4 slice. The times are simulated.
128 devices in a mesh: tm: 32 (over x, y, z_hi), tensor: 4 (over z_lo, core).
Axes of the slice: x: 4, y: 4, z: 4 (z_hi: 2, z_lo: 2; z = z_hi * 2 + z_lo), core: 2. Of those that a mesh axis runs over, the one named last changes fastest.
Arguments:
- frames: bfloat16 [16384, 1408], P('tm'), may hold values from -6 to 6
- gain_attn: float32 [1408], replicated, may hold values from 0.25 to 1.75
- w_qkv: bfloat16 [1408, 3, 1408], P('tm', None, 'tensor')
- w_out: bfloat16 [1408, 1408], P('tensor', 'tm'), may hold values from -0.625 to 0.625
- gain_mlp: float32 [1408], replicated, may hold values from 0.25 to 1.75
- w_up: bfloat16 [1408, 6144], P('tm', 'tensor'), may hold values from -0.15625 to 0.15625
- w_down: bfloat16 [6144, 1408], P('tensor', 'tm'), may hold values from -0.078125 to 0.078125
- w_proj: bfloat16 [1408, 4096], P('tm', 'tensor'), may hold values from -0.15625 to 0.15625
- windows: int32 [256, 8], P('tm'), may hold values from 0 to 255, as said below
- pool_map: int32 [16384], P('tm'), may hold values from 0 to 15, as said below
- owners: int32 [4096, 1], P('tm'), may hold values from 0 to 31; in each aligned block of 128 rows (0 to 127, 128 to 255, ...) at most 8 rows name the same one
Outputs:
- received: bfloat16 [32, 256, 4096], P('tm', None, 'tensor')
Inputs may be any that keep to these rules, and one draw needn't show every extreme that they name: `windows`: row b lists 8 different blocks, each in the frame of block b or in the frame just before or just after it; frame f holds blocks 256 / 64 f onward. `pool_map`: in each aligned block of 64 patches every slot value is named by exactly 4 patches. `owners`: among the 128 rows of one index of tm no owner is named more than 8 times.
All inputs are finite; a program needn't handle non-finite values.
Results may differ from a plain program's by a relative error of at most 0.014.
The roundings to bfloat16 on the way count: a program that leaves them out, or rounds other values in their place, can miss the bound.
Values may be sent and summed in bfloat16 or wider, within the bound.
A program may use at most 64 MiB of HBM per device.

v0:
```python
import math
import jax
import jax.numpy as jnp
from jax import lax
from jax.sharding import PartitionSpec as P

D = 1408
HEADS = 16
PATCHES = 256
BLK = 64
WIN = 8
POOL = 4
eps = 1e-06


def with_halo(block, sides, width):
    for axis, dim in sides:
        count = lax.axis_size(axis)
        forward = [(i, i + 1) for i in range(count - 1)]
        backward = [(target, source) for source, target in forward]
        low = lax.ppermute(
            lax.slice_in_dim(block, block.shape[dim] - width, None, axis=dim), axis, forward
        )
        high = lax.ppermute(lax.slice_in_dim(block, 0, width, axis=dim), axis, backward)
        block = jnp.concatenate([low, block, high], axis=dim)
    return block


def layer_norm(values, scales):
    average = jnp.mean(values, axis=-1, keepdims=True)
    centred = values - average
    spread = jnp.mean(centred * centred, axis=-1, keepdims=True)
    return (centred * lax.rsqrt(spread + eps) * scales).astype(jnp.bfloat16)


def pool_rows(values, slot_map):
    block_count = values.shape[0] // BLK
    slot_ids = jnp.arange(BLK // POOL, dtype=jnp.int32)
    chooser = (slot_map.reshape(block_count, 1, BLK) == slot_ids[None, :, None]).astype(jnp.float32)
    summed = jnp.einsum(
        "bsp,bpd->bsd",
        chooser,
        values.reshape(block_count, BLK, values.shape[1]),
        precision=lax.Precision.HIGHEST,
    )
    return (
        (summed * (1.0 / POOL))
        .reshape(block_count * (BLK // POOL), values.shape[1])
        .astype(jnp.bfloat16)
    )


def tensor_total(term):
    return lax.psum(term.astype(jnp.bfloat16), "tensor").astype(jnp.float32)


def body(
    frames, gain_attn, w_qkv, w_out, gain_mlp, w_up, w_down, w_proj, windows, pool_map, owners
):
    row_count = frames.shape[0]
    query_blocks = row_count // BLK
    head_dim = D // HEADS
    full_qkv, full_out, full_up, full_down, full_proj = (
        lax.all_gather(w_qkv, "tm", axis=0, tiled=True),
        lax.all_gather(w_out, "tm", axis=1, tiled=True),
        lax.all_gather(w_up, "tm", axis=0, tiled=True),
        lax.all_gather(w_down, "tm", axis=1, tiled=True),
        lax.all_gather(w_proj, "tm", axis=0, tiled=True),
    )
    local_width = full_qkv.shape[2]
    heads_here = local_width // head_dim
    normed = layer_norm(frames.astype(jnp.float32), gain_attn)
    projected_qkv = jnp.dot(
        normed, full_qkv.reshape(D, 3 * local_width), preferred_element_type=jnp.float32
    ).astype(jnp.bfloat16)
    projected_qkv = projected_qkv.reshape(row_count, 3, local_width)
    keyvals = with_halo(projected_qkv[:, 1:, :], (("tm", 0),), PATCHES)
    per_frame = PATCHES // BLK
    kv_blocks = keyvals.reshape(query_blocks + 2 * per_frame, BLK, 2, heads_here, head_dim)
    local_ids = windows - (lax.axis_index("tm") * query_blocks - per_frame)
    group_size = math.gcd(query_blocks, 8)
    queries = projected_qkv[:, 0, :].reshape(
        query_blocks // group_size, group_size, BLK, heads_here, head_dim
    )
    score_scale = head_dim ** (-0.5)

    def attend_group(packed):
        query_group, id_group = packed
        picked = kv_blocks[id_group].reshape(group_size, WIN * BLK, 2, heads_here, head_dim)
        scores = (
            jnp.einsum(
                "gqhd,gkhd->ghqk", query_group, picked[:, :, 0], preferred_element_type=jnp.float32
            )
            * score_scale
        )
        row_top = jnp.max(scores, axis=-1, keepdims=True)
        expw = jnp.exp(scores - row_top)
        attn_probs = (expw / jnp.sum(expw, axis=-1, keepdims=True)).astype(jnp.bfloat16)
        return jnp.einsum(
            "ghqk,gkhd->gqhd", attn_probs, picked[:, :, 1], preferred_element_type=jnp.float32
        ).astype(jnp.bfloat16)

    attended = lax.map(
        attend_group, (queries, local_ids.reshape(query_blocks // group_size, group_size, WIN))
    ).reshape(row_count, local_width)
    mixed_term = jnp.dot(attended, full_out, preferred_element_type=jnp.float32)
    stream = frames.astype(jnp.float32) + tensor_total(mixed_term)
    hidden = layer_norm(stream, gain_mlp)
    activation = jax.nn.gelu(
        jnp.dot(hidden, full_up, preferred_element_type=jnp.float32), approximate=False
    ).astype(jnp.bfloat16)
    stream = stream + tensor_total(
        jnp.dot(activation, full_down, preferred_element_type=jnp.float32)
    )
    pooled = pool_rows(stream, pool_map)
    proj_rows = jnp.dot(pooled, full_proj, preferred_element_type=jnp.float32).astype(jnp.bfloat16)
    pooled_count = proj_rows.shape[0]
    owner_count = lax.axis_size("tm")
    capacity = 2 * pooled_count // owner_count
    owner_ids = owners[:, 0]
    owner_hits = (owner_ids[:, None] == jnp.arange(owner_count, dtype=jnp.int32)[None, :]).astype(
        jnp.int32
    )
    slot_rank = jnp.sum((jnp.cumsum(owner_hits, axis=0) - 1) * owner_hits, axis=1)
    slot_dest = owner_ids * capacity + slot_rank
    placement = (
        jnp.arange(owner_count * capacity, dtype=jnp.int32)[:, None] == slot_dest[None, :]
    ).astype(jnp.bfloat16)
    outbox = jnp.dot(placement, proj_rows, preferred_element_type=jnp.float32).astype(jnp.bfloat16)
    outbox = outbox.reshape(owner_count, capacity, proj_rows.shape[1])
    received = lax.all_to_all(outbox, "tm", split_axis=0, concat_axis=0, tiled=True)
    return received.reshape(1, owner_count * capacity, proj_rows.shape[1])


def solution(mesh):
    placed = (
        P("tm", None),
        P(),
        P("tm", None, "tensor"),
        P("tensor", "tm"),
        P(),
        P("tm", "tensor"),
        P("tensor", "tm"),
        P("tm", "tensor"),
        P("tm", None),
        P("tm"),
        P("tm", None),
    )
    return jax.shard_map(
        body, mesh=mesh, in_specs=placed, out_specs=P("tm", None, "tensor"), check_vma=False
    )
```

profile of v0, /device:TPU:0, one launch (start us, length us, event | category | flops | bytes accessed | tf_op | source)
XLA Modules:
  0.0 647.8 jit_solution(6431842312539559043)
XLA Ops:
  6.5 1.6 copy.23
  8.1 0.0 all-gather.9.cloned.1.call-update
  8.2 0.0 all-reduce.3.cloned.1.call-start
  8.2 0.7 compare_select_fusion
  8.9 0.1 reshape.80
  9.0 1.6 convert_reduce_fusion
  10.6 1.9 fusion.16
  12.5 83.1 %all-gather.9.cloned.1.call-done = bf16[1408,3,352]{2,1,0:T(4,128)(2,1)} async-done(((bf16[44,3,352]{2,1,0:T(4,128)(2,1)}), bf16[1408,3,352]{2,1,0:T(4,128)(2,1)}) %all-gather.9.cloned.1.call-update) | async-done | bytes 2973712 | tf_op jit(solution)/shard_map/all_gather | solution.py:64
  95.6 7.7 %copy.24 = bf16[1408,3,352]{0,2,1:T(8,128)(2,1)} copy(bf16[1408,3,352]{2,1,0:T(4,128)(2,1)} %all-gather.9.cloned.1.call-done) | data formatting | bytes 5947392 | tf_op jit(solution)/shard_map/all_gather | solution.py:64
  103.3 3.9 convolution_convert_fusion.2
  107.2 1.0 copy-done.4
  108.2 0.2 copy.35
  108.4 2.3 collective-permute-start
  110.8 0.9 copy.37
  111.7 1.3 collective-permute-start.1
  113.0 102.0 %all-gather = bf16[32,44,352]{2,1,0:T(8,128)(2,1)S(1)} all-gather(bf16[1,44,352]{2,1,0:T(8,128)(2,1)S(1)} %bitcast.53), channel_id=1, replica_groups=mesh['tm'=32,'tensor'=4] {'tm'}, dimensions={0}, use_global_device_ids=true | all-gather | bytes 1022208 | tf_op jit(solution)/shard_map/all_gather | solution.py:65
  215.0 1.2 reshape.90
  216.2 1.2 slice.31
  217.3 1.0 slice.34
  218.3 1.2 copy.36
  219.5 1.3 reshape.97
  220.8 1.4 pad_maximum_fusion
  222.2 2.3 reshape.72
  224.5 2.1 copy.28
  226.6 5.5 gather_fusion
  232.2 9.4 %copy.29 = bf16[64,64,2,4,88]{4,1,0,3,2:T(8,128)(2,1)} copy(bf16[64,64,2,4,88]{4,1,3,2,0:T(8,128)(2,1)} %gather_fusion) | data formatting | bytes 11534336 | tf_op jit(solution)/shard_map/while/body/eval_jaxpr/gather | solution.py:89
  241.5 5.9 fusion.110
  247.4 6.2 copy.40
  253.6 2.6 fusion.19
  256.2 2.8 fusion.112
  259.0 6.1 copy.38
  265.1 4.4 fusion.72
  269.5 0.4 copy.34
  270.0 0.4 reshape.74
  270.3 2.0 convolution_convert_fusion.1
  272.4 0.0 all-reduce.3.cloned.1.call-update
  272.4 0.0 all-gather.11.cloned.1.call-start
  272.4 0.7 all-gather.11.cloned.1.call-update
  273.1 0.0 all-gather.13.cloned.1.call-start
  273.2 0.5 all-gather.13.cloned.1.call-update
  273.7 0.0 all-gather.15.cloned.1.call-start
  273.7 0.5 all-gather.15.cloned.1.call-update
  274.3 0.3 all-reduce.5.cloned.1.call-start
  274.6 41.4 %all-reduce.3.cloned.1.call-done = bf16[512,1408]{1,0:T(8,128)(2,1)} async-done(((bf16[512,1408]{1,0:T(8,128)(2,1)}), bf16[512,1408]{1,0:T(8,128)(2,1)}) %all-reduce.3.cloned.1.call-update) | async-done | bytes 1441808 | tf_op jit(solution)/shard_map/psum | solution.py:54
  315.9 1.9 fusion.24
  317.9 0.6 multiply_reduce_fusion.1
  318.5 86.1 %all-gather.11.cloned.1.call-done = bf16[32,44,1536]{2,1,0:T(8,128)(2,1)} async-done(((bf16[1,44,1536]{2,1,0:T(8,128)(2,1)}), bf16[32,44,1536]{2,1,0:T(8,128)(2,1)}) %all-gather.11.cloned.1.call-update) | async-done | bytes 4325392 | tf_op jit(solution)/shard_map/all_gather | solution.py:66
  404.6 7.0 %reshape.92 = bf16[1408,1536]{1,0:T(8,128)(2,1)} reshape(bf16[32,44,1536]{2,1,0:T(8,128)(2,1)} %all-gather.11.cloned.1.call-done) | data formatting | bytes 8650752
  411.7 77.3 %all-gather.13.cloned.1.call-done = bf16[32,44,1536]{2,1,0:T(8,128)(2,1)} async-done(((bf16[1,44,1536]{2,1,0:T(8,128)(2,1)}), bf16[32,44,1536]{2,1,0:T(8,128)(2,1)}) %all-gather.13.cloned.1.call-update) | async-done | bytes 4325392 | tf_op jit(solution)/shard_map/all_gather | solution.py:67
  488.9 7.0 %reshape.94 = bf16[1408,1536]{1,0:T(8,128)(2,1)} reshape(bf16[32,44,1536]{2,1,0:T(8,128)(2,1)} %all-gather.13.cloned.1.call-done) | data formatting | bytes 8650752
  496.0 15.1 %convolution_convert_fusion = bf16[512,1408]{1,0:T(8,128)(2,1)} fusion(bf16[1408,1536]{1,0:T(8,128)(2,1)} %reshape.94, bf16[1408,1536]{1,0:T(8,128)(2,1)} %reshape.92, bf16[512,1408]{1,0:T(8,128)(2,1)S(1)} %copy-done.1, bf16[512,1408]{1,0:T(8,128)(2,1)S(1)} %copy-done, f32[1408]{0:T(1024)S(1)} %copy-done.9, f32[512]{0:T(512)S(1)} %add_rsqrt_fusion, ...), kind=kOutput, calls=%fused_computation.30 | convolution fusion | flops 4486070272 | bytes 12985856 | tf_op jit(solution)/shard_map/dot_general | solution.py:113
  511.0 0.0 all-reduce.5.cloned.1.call-update
  511.1 0.1 eq.47
  511.2 0.1 fusion.77
  511.2 0.2 reduce_window_sum.11
  511.4 0.2 select_reduce_fusion
  511.6 54.0 %all-gather.15.cloned.1.call-done = bf16[32,44,1024]{2,1,0:T(8,128)(2,1)} async-done(((bf16[1,44,1024]{2,1,0:T(8,128)(2,1)}), bf16[32,44,1024]{2,1,0:T(8,128)(2,1)}) %all-gather.15.cloned.1.call-update) | async-done | bytes 2883600 | tf_op jit(solution)/shard_map/all_gather | solution.py:68
  565.6 5.2 reshape.96
  570.8 40.6 %all-reduce.5.cloned.1.call-done = bf16[512,1408]{1,0:T(8,128)(2,1)} async-done(((bf16[512,1408]{1,0:T(8,128)(2,1)}), bf16[512,1408]{1,0:T(8,128)(2,1)}) %all-reduce.5.cloned.1.call-update) | async-done | bytes 1441808 | tf_op jit(solution)/shard_map/psum | solution.py:54
  611.5 1.8 convert_add_fusion.1
  613.3 1.1 fusion.23
  614.4 2.6 fusion.71
  617.0 23.1 %all_to_all.5 = bf16[32,8,1024]{2,1,0:T(8,128)(2,1)S(1)} all-to-all(bf16[32,8,1024]{2,1,0:T(8,128)(2,1)S(1)} %fusion.71), channel_id=1, replica_groups=mesh['tm'=32,'tensor'=4] {'tm'}, dimensions={0} | all-to-all | bytes 1048576 | tf_op jit(solution)/shard_map/all_to_all | solution.py:131
  640.1 0.8 copy.48
  (29 shorter events, 0.1 us)
Async XLA Ops:
  6.5 89.1 %all-gather.9.cloned.1.call-start = ((), (), s32[]{:S(2)}) async-start(), calls=%async_computation.1 | async-start | bytes 4460544 | tf_op jit(solution)/shard_map/all_gather | solution.py:64
  8.2 307.8 %all-reduce.3.cloned.1.call-start = ((), (), s32[]{:S(2)}) async-start(), calls=%async_computation.2 | async-start | bytes 2883584 | tf_op jit(solution)/shard_map/psum | solution.py:54
  12.5 90.8 %copy-start = (bf16[512,1408]{1,0:T(8,128)(2,1)S(1)}, bf16[512,1408]{1,0:T(8,128)(2,1)}, u32[]{:S(2)}) copy-start(bf16[512,1408]{1,0:T(8,128)(2,1)} %param.11) | copy-start | bytes 4325380
  12.5 90.8 %copy-start.8 = (f32[1408]{0:T(1024)S(1)}, f32[1408]{0:T(1024)}, u32[]{:S(2)}) copy-start(f32[1408]{0:T(1024)} %param.12) | copy-start | bytes 16900
  103.3 9.7 %copy-start.5 = (bf16[352,44]{0,1:T(8,128)(2,1)S(1)}, bf16[352,44]{0,1:T(8,128)(2,1)}, u32[]{:S(2)}) copy-start(bf16[352,44]{0,1:T(8,128)(2,1)} %param.14) | copy-start | bytes 92932
  107.2 1.0 copy-start.4
  108.4 112.3 %collective-permute-start = (bf16[256,2,352]{2,0,1:T(8,128)(2,1)S(1)}, bf16[256,2,352]{2,0,1:T(8,128)(2,1)S(1)}, u32[]{:S(2)}, u32[]{:S(2)}) collective-permute-start(bf16[256,2,352]{2,0,1:T(8,128)(2,1)S(1)} %copy.35), channel_id=1, source_target_pairs={{0,4},{4,8},{8,12},{12,16},{16,20},{20,24},{24,28},{28,32},{32,36}... | collective-permute-start | bytes 1081352 | tf_op jit(solution)/shard_map/ppermute | solution.py:21
  111.7 109.1 %collective-permute-start.1 = (bf16[256,2,352]{2,0,1:T(8,128)(2,1)}, bf16[256,2,352]{2,0,1:T(8,128)(2,1)}, u32[]{:S(2)}, u32[]{:S(2)}) collective-permute-start(bf16[256,2,352]{2,0,1:T(8,128)(2,1)} %copy.37), channel_id=1, source_target_pairs={{4,0},{8,4},{12,8},{16,12},{20,16},{24,20},{28,24},{32,28},{36,32}... | collective-permute-start | bytes 1081352 | tf_op jit(solution)/shard_map/ppermute | solution.py:24
  247.4 6.2 copy-start.2
  265.1 5.2 copy-start.3
  272.4 132.2 %all-gather.11.cloned.1.call-start = ((), (), s32[]{:S(2)}) async-start(), calls=%async_computation.4 | async-start | bytes 4866048 | tf_op jit(solution)/shard_map/all_gather | solution.py:66
  273.1 215.8 %all-gather.13.cloned.1.call-start = ((), (), s32[]{:S(2)}) async-start(), calls=%async_computation.5 | async-start | bytes 4866048 | tf_op jit(solution)/shard_map/all_gather | solution.py:67
  273.7 291.9 %all-gather.15.cloned.1.call-start = ((), (), s32[]{:S(2)}) async-start(), calls=%async_computation.6 | async-start | bytes 3244032 | tf_op jit(solution)/shard_map/all_gather | solution.py:68
  274.3 337.2 %all-reduce.5.cloned.1.call-start = ((), (), s32[]{:S(2)}) async-start(), calls=%async_computation.3 | async-start | bytes 2883584 | tf_op jit(solution)/shard_map/psum | solution.py:54
  315.9 1.9 copy-start.1
  411.7 84.3 %copy-start.9 = (f32[1408]{0:T(1024)S(1)}, f32[1408]{0:T(1024)}, u32[]{:S(2)}) copy-start(f32[1408]{0:T(1024)} %param.15) | copy-start | bytes 16900
  496.0 15.1 %copy-start.7 = (s32[512]{0:T(512)S(1)}, s32[512]{0:T(512)}, u32[]{:S(2)}) copy-start(s32[512]{0:T(512)} %param.20) | copy-start | bytes 6148
  496.0 15.2 %copy-start.6 = (s32[128,1]{0,1:T(1,128)S(1)}, s32[128,1]{0,1:T(1,128)}, u32[]{:S(2)}) copy-start(s32[128,1]{0,1:T(1,128)} %param.21) | copy-start | bytes 1540
Sparse Core Ops, SparseCore 0:
  10.3 85.2 all-gather.8
  272.5 43.3 all-reduce.2
  318.9 85.6 all-gather.10
  407.4 81.4 all-gather.12
  491.7 73.8 all-gather.14
  568.0 43.4 all-reduce.4
where the time goes:
time: 649 us; the launch traced here: 648 us
  waiting for transfers between devices  384 us (59%)
  blocking collectives  125 us (19%)
  local copies, waits for them, and re-layouts  75.8 us (12%)
  matrix products  31.7 us (5%)
  between operations  13.7 us (2%)
  other arithmetic  13.3 us (2%)
    all_gather x1, blocking collectives, body(): lax.all_gather(w_out, 'tm', axis=1, tiled=True)  102 us
    all_gather x1, waiting for transfers between devices, body(): lax.all_gather(w_up, 'tm', axis=0, tiled=True)  86.1 us
    all_gather x1, waiting for transfers between devices, body(): lax.all_gather(w_qkv, 'tm', axis=0, tiled=True)  83.1 us
    psum x2, waiting for transfers between devices, tensor_total(): return lax.psum(term.astype(jnp.bfloat16), 'tensor').astype(jnp.float32)  82 us
    all_gather x1, waiting for transfers between devices, body(): lax.all_gather(w_down, 'tm', axis=1, tiled=True)  77.3 us
    all_gather x1, waiting for transfers between devices, body(): lax.all_gather(w_proj, 'tm', axis=0, tiled=True)  54 us
    unnamed x31, local copies, waits for them, and re-layouts  38.5 us
    all_to_all x1, blocking collectives, body(): lax.all_to_all(outbox, 'tm', split_axis=0, concat_axis=0, tiled=True)  23.1 us
  transfers between devices with their start and end apart: 8, of which 6 were waited for; matrix products, arithmetic and copies ran while one was open for 7% of the time, Pallas kernels for 0%

commit v1 on v0

--- a/solution.py
+++ b/solution.py
@@ -61,7 +61,9 @@
     query_blocks = row_count // BLK
     head_dim = D // HEADS
     full_qkv, full_out, full_up, full_down, full_proj = (
-        lax.all_gather(w_qkv, "tm", axis=0, tiled=True),
+        jnp.concatenate(
+            lax.all_to_all(jnp.stack([w_qkv] * lax.axis_size("tm")), "tm", 0, 0), axis=0
+        ),
         lax.all_gather(w_out, "tm", axis=1, tiled=True),
         lax.all_gather(w_up, "tm", axis=0, tiled=True),
         lax.all_gather(w_down, "tm", axis=1, tiled=True),

time: 649 us -> 540 us (0.83)
  waiting for transfers between devices: 384 us -> 263 us
  starting transfers between devices: 4.01 us -> 15.9 us
  local copies, waits for them, and re-layouts: 75.8 us -> 84 us
    all_gather x1 -> x0, waiting for transfers between devices: 83.1 us -> none  [body(): lax.all_gather(w_qkv, 'tm', axis=0, tiled=True)]
    all_gather x1, waiting for transfers between devices: 86.1 us -> 35.9 us  [body(): lax.all_gather(w_up, 'tm', axis=0, tiled=True)]
    all_to_all x0 -> x1, waiting for transfers between devices: none -> 47.2 us  [body(): lax.all_to_all(jnp.stack([w_qkv] * lax.axis_size('tm')), 'tm', 0, 0)]
    psum x2, waiting for transfers between devices: 82 us -> 44.4 us  [tensor_total(): return lax.psum(term.astype(jnp.bfloat16), 'tensor').astype(jnp.float32)]
    another operation x0 -> x2, local copies, waits for them, and re-layouts: none -> 11.9 us  [the longest x1 8.92 us: body(): full_qkv.reshape(D, 3 * local_width)]
    all_to_all x0 -> x1, starting transfers between devices: none -> 11 us  [body(): lax.all_to_all(jnp.stack([w_qkv] * lax.axis_size('tm')), 'tm', 0, 0)]
    all_gather x1 -> x0, local copies, waits for them, and re-layouts: 7.69 us -> none  [body(): lax.all_gather(w_qkv, 'tm', axis=0, tiled=True)]
    unnamed x31 -> x32, local copies, waits for them, and re-layouts: 38.5 us -> 36.9 us
  transfers between devices with their start and end apart: 8 -> 8, of which waited for: 6 -> 5; matrix products, arithmetic and copies ran while one was open for 7% -> 8% of each run, Pallas kernels for 0% -> 0%
where the time goes in v1:
time: 540 us; the launch traced here: 539 us
  waiting for transfers between devices  263 us (49%)
  blocking collectives  119 us (22%)
  local copies, waits for them, and re-layouts  84 us (16%)
  matrix products  31.8 us (6%)
  starting transfers between devices  15.9 us (3%)
  between operations  15.2 us (3%)
  other arithmetic  9.91 us (2%)
    all_gather x1, blocking collectives, body(): lax.all_gather(w_out, 'tm', axis=1, tiled=True)  102 us
    all_gather x1, waiting for transfers between devices, body(): lax.all_gather(w_down, 'tm', axis=1, tiled=True)  77.2 us
    all_gather x1, waiting for transfers between devices, body(): lax.all_gather(w_proj, 'tm', axis=0, tiled=True)  56.6 us
    all_to_all x1, waiting for transfers between devices, body(): lax.all_to_all(jnp.stack([w_qkv] * lax.axis_size('tm')), 'tm', 0, 0)  47.2 us
    psum x2, waiting for transfers between devices, tensor_total(): return lax.psum(term.astype(jnp.bfloat16), 'tensor').astype(jnp.float32)  44.4 us
    unnamed x32, local copies, waits for them, and re-layouts  36.9 us
    all_gather x1, waiting for transfers between devices, body(): lax.all_gather(w_up, 'tm', axis=0, tiled=True)  35.9 us
    all_to_all x1, blocking collectives, body(): lax.all_to_all(outbox, 'tm', split_axis=0, concat_axis=0, tiled=True)  17 us
  transfers between devices with their start and end apart: 8, of which 5 were waited for; matrix products, arithmetic and copies ran while one was open for 8% of the time, Pallas kernels for 0%

profile of v1, /device:TPU:0, one launch (start us, length us, event | category | flops | bytes accessed | tf_op | source)
XLA Modules:
  0.0 538.6 jit_solution(12738173939977438523)
XLA Ops:
  7.4 2.9 stack.2
  10.3 11.0 %all-to-all-start = ((bf16[32,44,3,352]{3,1,2,0:T(8,128)(2,1)}), bf16[32,44,3,352]{3,1,2,0:T(8,128)(2,1)}, u32[]{:S(2)}, u32[]{:S(2)}) async-start(bf16[32,44,3,352]{3,1,2,0:T(8,128)(2,1)} %stack.2), calls=%async_computation | async-start | bytes 7077888 | tf_op jit(solution)/shard_map/all_to_all | solution.py:65
  21.3 0.0 all-reduce.3.cloned.1.call-start
  21.4 0.1 reshape.78
  21.5 0.3 convert_reduce_fusion
  21.7 0.5 fusion.16
  22.3 47.2 %all-to-all-done = bf16[32,44,3,352]{3,1,2,0:T(8,128)(2,1)} async-done(((bf16[32,44,3,352]{3,1,2,0:T(8,128)(2,1)}), bf16[32,44,3,352]{3,1,2,0:T(8,128)(2,1)}, u32[]{:S(2)}, u32[]{:S(2)}) %all-to-all-start) | async-done | bytes 2973728 | tf_op jit(solution)/shard_map/all_to_all | solution.py:65
  69.5 5.7 %copy.24 = bf16[32,44,3,352]{3,2,1,0:T(4,128)(2,1)} copy(bf16[32,44,3,352]{3,1,2,0:T(8,128)(2,1)} %all-to-all-done) | data formatting | bytes 5947392 | tf_op jit(solution)/shard_map/all_to_all | solution.py:65
  75.2 8.9 %reshape_reshape.3 = bf16[1408,1056]{1,0:T(8,128)(2,1)} reshape(bf16[32,44,3,352]{3,2,1,0:T(4,128)(2,1)} %copy.24) | data formatting | bytes 5947392 | tf_op jit(solution)/shard_map/reshape;reshape | solution.py:76
  84.1 4.0 convolution_convert_fusion
  88.1 1.0 copy-done.4
  89.1 0.2 copy.35
  89.4 3.2 collective-permute-start
  92.6 0.9 copy.37
  93.5 1.3 collective-permute-start.1
  94.8 101.8 %all-gather = bf16[32,44,352]{2,1,0:T(8,128)(2,1)S(1)} all-gather(bf16[1,44,352]{2,1,0:T(8,128)(2,1)S(1)} %bitcast.51), channel_id=1, replica_groups=mesh['tm'=32,'tensor'=4] {'tm'}, dimensions={0}, use_global_device_ids=true | all-gather | bytes 1022208 | tf_op jit(solution)/shard_map/all_gather | solution.py:67
  196.7 1.2 reshape.88
  197.9 1.2 slice.31
  199.0 1.0 slice.34
  200.0 1.2 copy.36
  201.2 1.3 reshape.95
  202.5 0.0 collective-permute-done
  202.5 1.4 pad_maximum_fusion
  203.9 2.3 reshape.70
  206.2 2.1 copy.28
  208.3 5.5 %gather_fusion = bf16[64,64,2,4,88]{4,1,3,2,0:T(8,128)(2,1)} fusion(bf16[16,64,2,4,88]{4,1,3,2,0:T(8,128)(2,1)S(1)} %copy.28, s32[1024]{0:T(1024)S(1)} %pad_clamp_fusion), kind=kCustom, calls=%fused_computation | custom fusion | bytes 11534592 | tf_op jit(solution)/shard_map/while/body/eval_jaxpr/gather | solution.py:91
  213.9 9.4 %copy.29 = bf16[64,64,2,4,88]{4,1,0,3,2:T(8,128)(2,1)} copy(bf16[64,64,2,4,88]{4,1,3,2,0:T(8,128)(2,1)} %gather_fusion) | data formatting | bytes 11534336 | tf_op jit(solution)/shard_map/while/body/eval_jaxpr/gather | solution.py:91
  223.2 5.9 %fusion.110 = (bf16[8,512,1,4,88]{4,1,0,3,2:T(8,128)(2,1)}, bf16[8,512,1,4,88]{4,1,0,3,2:T(8,128)(2,1)}) fusion(bf16[8,512,2,4,88]{4,1,0,3,2:T(8,128)(2,1)} %bitcast.41), kind=kLoop, calls=%fused_computation.136 | loop fusion | bytes 11534336 | tf_op jit(solution)/shard_map/while/body/eval_jaxpr/slice | solution.py:102
  229.1 6.2 %copy.40 = bf16[8,512,1,4,88]{1,4,3,0,2:T(8,128)(2,1)} copy(bf16[8,512,1,4,88]{4,1,0,3,2:T(8,128)(2,1)} %get-tuple-element.14) | data formatting | bytes 5767168
  235.3 2.6 fusion.19
  237.9 2.8 fusion.112
  240.7 6.1 %copy.38 = bf16[8,512,1,4,88]{1,4,3,0,2:T(8,128)(2,1)} copy(bf16[8,512,1,4,88]{4,1,0,3,2:T(8,128)(2,1)} %get-tuple-element.13) | data formatting | bytes 5767168
  246.8 4.4 fusion.72
  251.2 0.4 copy.34
  251.6 0.4 reshape.72
  252.0 2.0 convolution_convert_fusion.2
  254.1 0.0 all-reduce.3.cloned.1.call-update
  254.1 0.0 all-gather.8.cloned.1.call-start
  254.1 0.5 all-gather.8.cloned.1.call-update
  254.7 0.0 all-gather.10.cloned.1.call-start
  254.7 0.5 all-gather.10.cloned.1.call-update
  255.3 0.0 all-gather.12.cloned.1.call-start
  255.3 0.5 all-gather.12.cloned.1.call-update
  255.8 0.3 all-reduce.5.cloned.1.call-start
  256.1 44.4 %all-reduce.3.cloned.1.call-done = bf16[512,1408]{1,0:T(8,128)(2,1)} async-done(((bf16[512,1408]{1,0:T(8,128)(2,1)}), bf16[512,1408]{1,0:T(8,128)(2,1)}) %all-reduce.3.cloned.1.call-update) | async-done | bytes 1441808 | tf_op jit(solution)/shard_map/psum | solution.py:54
  300.5 1.9 fusion.24
  302.4 0.6 multiply_reduce_fusion.1
  303.1 35.9 %all-gather.8.cloned.1.call-done = bf16[32,44,1536]{2,1,0:T(8,128)(2,1)} async-done(((bf16[1,44,1536]{2,1,0:T(8,128)(2,1)}), bf16[32,44,1536]{2,1,0:T(8,128)(2,1)}) %all-gather.8.cloned.1.call-update) | async-done | bytes 4325392 | tf_op jit(solution)/shard_map/all_gather | solution.py:68
  339.0 7.0 %reshape.90 = bf16[1408,1536]{1,0:T(8,128)(2,1)} reshape(bf16[32,44,1536]{2,1,0:T(8,128)(2,1)} %all-gather.8.cloned.1.call-done) | data formatting | bytes 8650752
  346.0 77.2 %all-gather.10.cloned.1.call-done = bf16[32,44,1536]{2,1,0:T(8,128)(2,1)} async-done(((bf16[1,44,1536]{2,1,0:T(8,128)(2,1)}), bf16[32,44,1536]{2,1,0:T(8,128)(2,1)}) %all-gather.10.cloned.1.call-update) | async-done | bytes 4325392 | tf_op jit(solution)/shard_map/all_gather | solution.py:69
  423.2 7.0 %reshape.92 = bf16[1408,1536]{1,0:T(8,128)(2,1)} reshape(bf16[32,44,1536]{2,1,0:T(8,128)(2,1)} %all-gather.10.cloned.1.call-done) | data formatting | bytes 8650752
  430.3 15.1 %convolution_convert_fusion.1 = bf16[512,1408]{1,0:T(8,128)(2,1)} fusion(bf16[1408,1536]{1,0:T(8,128)(2,1)} %reshape.92, bf16[1408,1536]{1,0:T(8,128)(2,1)} %reshape.90, bf16[512,1408]{1,0:T(8,128)(2,1)S(1)} %copy-done.1, bf16[512,1408]{1,0:T(8,128)(2,1)S(1)} %copy-done, f32[1408]{0:T(1024)S(1)} %copy-done.10, f32[512]{0:T(512)S(1)} %add_rsqrt_fusion, ...), kind=kOutput, calls=%fused_computation.31 | convolution fusion | flops 4486070272 | bytes 12985856 | tf_op jit(solution)/shard_map/dot_general | solution.py:115
  445.3 0.0 all-reduce.5.cloned.1.call-update
  445.4 0.1 eq.47
  445.4 0.1 fusion.77
  445.5 0.2 reduce_window_sum.11
  445.7 0.2 select_reduce_fusion
  445.9 56.6 %all-gather.12.cloned.1.call-done = bf16[32,44,1024]{2,1,0:T(8,128)(2,1)} async-done(((bf16[1,44,1024]{2,1,0:T(8,128)(2,1)}), bf16[32,44,1024]{2,1,0:T(8,128)(2,1)}) %all-gather.12.cloned.1.call-update) | async-done | bytes 2883600 | tf_op jit(solution)/shard_map/all_gather | solution.py:70
  502.4 5.2 reshape.94
  507.7 1.8 convert_add_fusion.1
  509.5 1.1 fusion.23
  510.6 2.6 fusion.71
  513.2 17.0 %all_to_all.10 = bf16[32,8,1024]{2,1,0:T(8,128)(2,1)S(1)} all-to-all(bf16[32,8,1024]{2,1,0:T(8,128)(2,1)S(1)} %fusion.71), channel_id=1, replica_groups=mesh['tm'=32,'tensor'=4] {'tm'}, dimensions={0} | all-to-all | bytes 1048576 | tf_op jit(solution)/shard_map/all_to_all | solution.py:133
  530.2 0.8 copy.48
  (31 shorter events, 0.1 us)
Async XLA Ops:
  10.3 11.1 %copy-start.6 = (s32[8,8]{1,0:T(8,128)S(1)}, s32[8,8]{1,0:T(8,128)}, u32[]{:S(2)}) copy-start(s32[8,8]{1,0:T(8,128)} %param.19) | copy-start | bytes 772
  10.3 11.2 %copy-start = (bf16[512,1408]{1,0:T(8,128)(2,1)S(1)}, bf16[512,1408]{1,0:T(8,128)(2,1)}, u32[]{:S(2)}) copy-start(bf16[512,1408]{1,0:T(8,128)(2,1)} %param.11) | copy-start | bytes 4325380
  10.3 59.2 %all-to-all-start = ((bf16[32,44,3,352]{3,1,2,0:T(8,128)(2,1)}), bf16[32,44,3,352]{3,1,2,0:T(8,128)(2,1)}, u32[]{:S(2)}, u32[]{:S(2)}) async-start(bf16[32,44,3,352]{3,1,2,0:T(8,128)(2,1)} %stack.2), calls=%async_computation | async-start | bytes 7077888 | tf_op jit(solution)/shard_map/all_to_all | solution.py:65
  21.3 279.1 %all-reduce.3.cloned.1.call-start = ((), (), s32[]{:S(2)}) async-start(), calls=%async_computation.2 | async-start | bytes 2883584 | tf_op jit(solution)/shard_map/psum | solution.py:54
  75.2 8.9 %copy-start.9 = (f32[1408]{0:T(1024)S(1)}, f32[1408]{0:T(1024)}, u32[]{:S(2)}) copy-start(f32[1408]{0:T(1024)} %param.12) | copy-start | bytes 16900
  84.1 10.7 %copy-start.5 = (bf16[352,44]{0,1:T(8,128)(2,1)S(1)}, bf16[352,44]{0,1:T(8,128)(2,1)}, u32[]{:S(2)}) copy-start(bf16[352,44]{0,1:T(8,128)(2,1)} %param.14) | copy-start | bytes 92932
  88.1 1.0 copy-start.4
  89.4 113.1 %collective-permute-start = (bf16[256,2,352]{2,0,1:T(8,128)(2,1)S(1)}, bf16[256,2,352]{2,0,1:T(8,128)(2,1)S(1)}, u32[]{:S(2)}, u32[]{:S(2)}) collective-permute-start(bf16[256,2,352]{2,0,1:T(8,128)(2,1)S(1)} %copy.35), channel_id=1, source_target_pairs={{0,4},{4,8},{8,12},{12,16},{16,20},{20,24},{24,28},{28,32},{32,36}... | collective-permute-start | bytes 1081352 | tf_op jit(solution)/shard_map/ppermute | solution.py:21
  93.5 109.0 %collective-permute-start.1 = (bf16[256,2,352]{2,0,1:T(8,128)(2,1)}, bf16[256,2,352]{2,0,1:T(8,128)(2,1)}, u32[]{:S(2)}, u32[]{:S(2)}) collective-permute-start(bf16[256,2,352]{2,0,1:T(8,128)(2,1)} %copy.37), channel_id=1, source_target_pairs={{4,0},{8,4},{12,8},{16,12},{20,16},{24,20},{28,24},{32,28},{36,32}... | collective-permute-start | bytes 1081352 | tf_op jit(solution)/shard_map/ppermute | solution.py:24
  229.1 6.2 %copy-start.2 = (bf16[8,64,4,88]{1,0,3,2:T(8,128)(2,1)S(1)}, bf16[8,64,4,88]{1,0,3,2:T(8,128)(2,1)}, u32[]{:S(2)}) copy-start(bf16[8,64,4,88]{1,0,3,2:T(8,128)(2,1)} %reshape.95) | copy-start | bytes 1081348
  246.8 5.2 copy-start.3
  254.1 84.9 %all-gather.8.cloned.1.call-start = ((), (), s32[]{:S(2)}) async-start(), calls=%async_computation.4 | async-start | bytes 4866048 | tf_op jit(solution)/shard_map/all_gather | solution.py:68
  254.7 168.6 %all-gather.10.cloned.1.call-start = ((), (), s32[]{:S(2)}) async-start(), calls=%async_computation.5 | async-start | bytes 4866048 | tf_op jit(solution)/shard_map/all_gather | solution.py:69
  255.3 247.2 %all-gather.12.cloned.1.call-start = ((), (), s32[]{:S(2)}) async-start(), calls=%async_computation.6 | async-start | bytes 3244032 | tf_op jit(solution)/shard_map/all_gather | solution.py:70
  255.8 251.9 %all-reduce.5.cloned.1.call-start = ((), (), s32[]{:S(2)}) async-start(), calls=%async_computation.3 | async-start | bytes 2883584 | tf_op jit(solution)/shard_map/psum | solution.py:54
  300.5 1.9 copy-start.1
  346.0 84.2 %copy-start.10 = (f32[1408]{0:T(1024)S(1)}, f32[1408]{0:T(1024)}, u32[]{:S(2)}) copy-start(f32[1408]{0:T(1024)} %param.15) | copy-start | bytes 16900
  430.2 15.1 %copy-start.8 = (s32[512]{0:T(512)S(1)}, s32[512]{0:T(512)}, u32[]{:S(2)}) copy-start(s32[512]{0:T(512)} %param.20) | copy-start | bytes 6148
  430.2 15.2 %copy-start.7 = (s32[128,1]{0,1:T(1,128)S(1)}, s32[128,1]{0,1:T(1,128)}, u32[]{:S(2)}) copy-start(s32[128,1]{0,1:T(1,128)} %param.21) | copy-start | bytes 1540
Sparse Core Ops, SparseCore 0:
  254.2 46.2 all-reduce.2
  445.5 55.9 all-reduce.4
Sparse Core Ops, SparseCore 1:
  257.5 81.4 all-gather.7
  341.8 81.4 all-gather.9
  426.1 76.3 all-gather.11
